TPU v7x, 128 devices: a whole 4x4x4 slice. The times are simulated.
128 devices in a mesh: row: 32 (over z, y, core), col: 4 (over x).
Axes of the slice: x: 4, y: 4, z: 4, core: 2. Of those that a mesh axis runs over, the one named last changes fastest.
Arguments:
- tokens: bfloat16 [16384, 2048], P('row', 'col'), may hold values from -6 to 6
- cotangent: bfloat16 [16384, 2048], P('row', 'col'), may hold values from -6 to 6
- destination: int32 [16384], P('row'), may hold values from 0 to 16383, as said below
- segment_ids: int32 [16384], P('row'), may hold values from 0 to 7, as said below
- attn_gain: float32 [2048], replicated, may hold values from 0.5 to 1.5
- w_query: bfloat16 [2048, 2048], P('row', 'col'), may hold values from -0.125 to 0.125
- w_key: bfloat16 [2048, 256], P('row', 'col'), may hold values from -0.125 to 0.125
- w_value: bfloat16 [2048, 256], P('row', 'col'), may hold values from -0.125 to 0.125
- w_output: bfloat16 [2048, 2048], P('row', 'col'), may hold values from -0.5 to 0.5
- ffn_gain: float32 [2048], replicated, may hold values from 0.5 to 1.5
- w_gate: bfloat16 [2048, 5632], P('row', 'col'), may hold values from -0.125 to 0.125
- w_up: bfloat16 [2048, 5632], P('row', 'col'), may hold values from -0.125 to 0.125
- w_down: bfloat16 [2048, 5632], P('row', 'col'), may hold values from -0.078125 to 0.078125
Outputs:
- output: bfloat16 [16384, 2048], P('row', 'col')
- input_grad: bfloat16 [16384, 2048], P('row', 'col')
- attn_gain_grad: float32 [2048], P('row')
- w_query_grad: float32 [2048, 2048], P('row', 'col')
- w_key_grad: float32 [2048, 256], P('row', 'col')
- w_value_grad: float32 [2048, 256], P('row', 'col')
- w_output_grad: float32 [2048, 2048], P('row', 'col')
- ffn_gain_grad: float32 [2048], P('row')
- w_gate_grad: float32 [2048, 5632], P('row', 'col')
- w_up_grad: float32 [2048, 5632], P('row', 'col')
- w_down_grad: float32 [2048, 5632], P('row', 'col')
Inputs may be any that keep to these rules, and one draw needn't show every extreme that they name: `destination`: A permutation; the tokens of each aligned block of 512 arriving tokens go to exactly 16 places in each aligned block of 512 balanced places. `segment_ids`: within each aligned block of 512 places the ids start at 0 and rise by one where a new sequence begins, so a block holds at most 8 sequences; in every draw some block holds a single sequence of 512 tokens and some block holds 8 sequences.
All inputs are finite; a program needn't handle non-finite values.
Results may differ from a plain program's by a relative error of at most 0.028.
Values may be sent and summed in bfloat16 or wider, within the bound.
No kernel may reach another device: no remote copies, remote signals or barrier semaphores. Data moves between devices by JAX's collectives and lax.ppermute only.
A program may use at most 128 MiB of HBM per device.

v0:
```python
from functools import partial
import jax
import jax.numpy as jnp
from jax import lax
from jax.sharding import PartitionSpec as P

HEADS = 32
KV = 4
HD = 64
EPS = 1e-05
ROPE_BASE = 10000.0


def rope_tables(positions):
    half_width = HD // 2
    freqs = ROPE_BASE ** (-(jnp.arange(half_width, dtype=jnp.float32) * 2.0 / HD))
    angles = positions.astype(jnp.float32)[:, None] * freqs[None, :]
    return (jnp.cos(angles)[:, None, :], jnp.sin(angles)[:, None, :])


def rotate(values, cosine, sine):
    half_width = values.shape[-1] // 2
    first = values[..., :half_width]
    second = values[..., half_width:]
    return jnp.concatenate(
        [first * cosine - second * sine, second * cosine + first * sine], axis=-1
    )


def rotate_back(grads, cosine, sine):
    half_width = grads.shape[-1] // 2
    first = grads[..., :half_width]
    second = grads[..., half_width:]
    return jnp.concatenate(
        [first * cosine + second * sine, second * cosine - first * sine], axis=-1
    )


def positions_of(segment_ids):
    index = jnp.arange(segment_ids.shape[0], dtype=jnp.int32)
    change = jnp.concatenate([jnp.ones((1,), dtype=jnp.bool_), segment_ids[1:] != segment_ids[:-1]])
    starts = jnp.where(change, index, jnp.zeros_like(index))
    return index - lax.cummax(starts, axis=0)


def allowed_pairs(segment_ids):
    index = jnp.arange(segment_ids.shape[0], dtype=jnp.int32)
    return (segment_ids[:, None] == segment_ids[None, :]) & (index[None, :] <= index[:, None])


def rms_scale(values):
    return lax.rsqrt(jnp.mean(values * values, axis=-1, keepdims=True) + EPS)


def norm_back(values, inv_root, gain, grads):
    normed = values * inv_root
    scaled = grads * gain
    result = inv_root * (scaled - normed * jnp.mean(scaled * normed, axis=-1, keepdims=True))
    return (result, jnp.sum(grads * normed, axis=0))


def matmul(left, right):
    return jnp.dot(left, right, preferred_element_type=jnp.float32)


def head_scores(query_head, key_head, allowed, scale_factor):
    scores = matmul(query_head, key_head.T) * scale_factor
    return jnp.where(allowed, scores, -1e30)


def head_forward(inputs, key_heads, value_heads, allowed, scale_factor):
    query_head, kv_slot = inputs
    scores = head_scores(query_head, key_heads[kv_slot], allowed, scale_factor)
    peak = jnp.max(scores, axis=-1, keepdims=True)
    expo = jnp.exp(scores - peak)
    total = jnp.sum(expo, axis=-1, keepdims=True)
    probs = expo / total
    mixed = matmul(probs.astype(jnp.bfloat16), value_heads[kv_slot])
    return (mixed, (peak + jnp.log(total))[:, 0])


def head_backward(inputs, key_heads, value_heads, allowed, scale_factor):
    query_head, kv_slot, grad_head, log_total = inputs
    key_head = key_heads[kv_slot]
    value_head = value_heads[kv_slot]
    scores = head_scores(query_head, key_head, allowed, scale_factor)
    probs = jnp.exp(scores - log_total[:, None])
    prob_grad = matmul(grad_head, value_head.T)
    value_grad = matmul(probs.astype(jnp.bfloat16).T, grad_head)
    inner = jnp.sum(probs * prob_grad, axis=-1, keepdims=True)
    score_grad = (probs * (prob_grad - inner)).astype(jnp.bfloat16)
    query_grad = matmul(score_grad, key_head) * scale_factor
    key_grad = matmul(score_grad.T, query_head) * scale_factor
    return (query_grad, key_grad, value_grad)


def gather_rows(parts):
    widths = [part.shape[1] for part in parts]
    packed = lax.all_gather(jnp.concatenate(parts, axis=1), "row", axis=0, tiled=True)
    pieces = []
    offset = 0
    for width in widths:
        pieces.append(packed[:, offset : offset + width])
        offset += width
    return pieces


def scatter_rows(parts):
    columns = [part.reshape(part.shape[0], -1).astype(jnp.bfloat16) for part in parts]
    widths = [column.shape[1] for column in columns]
    packed = lax.psum_scatter(
        jnp.concatenate(columns, axis=1), "row", scatter_dimension=0, tiled=True
    ).astype(jnp.float32)
    pieces = []
    offset = 0
    for part, width in zip(parts, widths):
        piece = packed[:, offset : offset + width]
        pieces.append(piece.reshape(-1) if part.ndim == 1 else piece)
        offset += width
    return pieces


def body(
    tokens,
    cotangent,
    destination,
    segment_ids,
    attn_gain,
    w_query,
    w_key,
    w_value,
    w_output,
    ffn_gain,
    w_gate,
    w_up,
    w_down,
):
    row_count = tokens.shape[0]
    quarter = tokens.shape[1]
    col_start = lax.axis_index("col") * quarter
    group_size = HEADS // KV
    send_order = jnp.argsort(destination)
    slot_ids = destination[send_order] % row_count
    arrived_rows, arrived_grads, arrived_slots = (
        lax.all_to_all(tokens[send_order], "row", split_axis=0, concat_axis=0, tiled=True),
        lax.all_to_all(cotangent[send_order], "row", split_axis=0, concat_axis=0, tiled=True),
        lax.all_to_all(slot_ids, "row", split_axis=0, concat_axis=0, tiled=True),
    )
    placing = jnp.argsort(arrived_slots)
    full_rows, full_grads = (
        lax.all_gather(arrived_rows[placing], "col", axis=1, tiled=True),
        lax.all_gather(arrived_grads[placing], "col", axis=1, tiled=True),
    )
    query_w, key_w, value_w, output_w = gather_rows([w_query, w_key, w_value, w_output])
    cosine, sine = rope_tables(positions_of(segment_ids))
    allowed = allowed_pairs(segment_ids)
    rows_wide = full_rows.astype(jnp.float32)
    inv_one = rms_scale(rows_wide)
    normed_one = (rows_wide * inv_one * attn_gain).astype(jnp.bfloat16)
    query = matmul(normed_one, query_w)
    key_raw = matmul(normed_one, key_w)
    value_raw = matmul(normed_one, value_w)
    query_heads_count = query.shape[1] // HD
    kv_count = key_raw.shape[1] // HD
    query_rot = (
        rotate(query.reshape(row_count, query_heads_count, HD), cosine, sine)
        .astype(jnp.bfloat16)
        .transpose(1, 0, 2)
    )
    key_rot = (
        rotate(key_raw.reshape(row_count, kv_count, HD), cosine, sine)
        .astype(jnp.bfloat16)
        .transpose(1, 0, 2)
    )
    value_heads = value_raw.astype(jnp.bfloat16).reshape(row_count, kv_count, HD).transpose(1, 0, 2)
    kv_slots = jnp.arange(query_heads_count, dtype=jnp.int32) // group_size
    scale_factor = HD ** (-0.5)
    mixed_heads, log_totals = lax.map(
        partial(
            head_forward,
            key_heads=key_rot,
            value_heads=value_heads,
            allowed=allowed,
            scale_factor=scale_factor,
        ),
        (query_rot, kv_slots),
    )
    mixed = (
        mixed_heads.transpose(1, 0, 2)
        .reshape(row_count, query_heads_count * HD)
        .astype(jnp.bfloat16)
    )
    attn_terms = matmul(mixed, output_w.T)
    attn_full = lax.psum(attn_terms, "col")
    resid = rows_wide + attn_full
    inv_two = rms_scale(resid)
    normed_two = (resid * inv_two * ffn_gain).astype(jnp.bfloat16)
    resid_part = lax.dynamic_slice_in_dim(resid, col_start, quarter, 1)
    gate_w, up_w, down_w = gather_rows([w_gate, w_up, w_down])
    gate = matmul(normed_two, gate_w)
    upper = matmul(normed_two, up_w)
    sigmoid_gate = jax.nn.sigmoid(gate)
    activ = (gate * sigmoid_gate * upper).astype(jnp.bfloat16)
    ffn_share = lax.psum_scatter(
        matmul(activ, down_w.T).astype(jnp.bfloat16), "col", scatter_dimension=1, tiled=True
    ).astype(jnp.float32)
    output_share = (resid_part + ffn_share).astype(jnp.bfloat16)
    down_weight_grad = matmul(full_grads.T, activ)
    act_grad = matmul(full_grads, down_w)
    gate_grad = (act_grad * upper * sigmoid_gate * (1.0 + gate * (1.0 - sigmoid_gate))).astype(
        jnp.bfloat16
    )
    up_grad = (act_grad * gate * sigmoid_gate).astype(jnp.bfloat16)
    gate_weight_grad = matmul(normed_two.T, gate_grad)
    up_weight_grad = matmul(normed_two.T, up_grad)
    normed_terms_two = matmul(gate_grad, gate_w.T) + matmul(up_grad, up_w.T)
    normed_grad_two = lax.psum(normed_terms_two, "col")
    resid_norm_grad, ffn_gain_grad = norm_back(resid, inv_two, ffn_gain, normed_grad_two)
    resid_grad = full_grads.astype(jnp.float32) + resid_norm_grad
    attn_grad_low = resid_grad.astype(jnp.bfloat16)
    output_weight_grad = matmul(attn_grad_low.T, mixed)
    mixed_grad = matmul(attn_grad_low, output_w).astype(jnp.bfloat16)
    mixed_grad_heads = mixed_grad.reshape(row_count, query_heads_count, HD).transpose(1, 0, 2)
    query_grads, key_grads, value_grads = lax.map(
        partial(
            head_backward,
            key_heads=key_rot,
            value_heads=value_heads,
            allowed=allowed,
            scale_factor=scale_factor,
        ),
        (query_rot, kv_slots, mixed_grad_heads, log_totals),
    )
    query_grad = (
        rotate_back(query_grads.transpose(1, 0, 2), cosine, sine)
        .reshape(row_count, query_heads_count * HD)
        .astype(jnp.bfloat16)
    )
    key_sum = key_grads.reshape(kv_count, group_size, row_count, HD).sum(axis=1).transpose(1, 0, 2)
    key_grad = (
        rotate_back(key_sum, cosine, sine).reshape(row_count, kv_count * HD).astype(jnp.bfloat16)
    )
    value_sum = (
        value_grads.reshape(kv_count, group_size, row_count, HD).sum(axis=1).transpose(1, 0, 2)
    )
    value_grad = value_sum.reshape(row_count, kv_count * HD).astype(jnp.bfloat16)
    query_weight_grad = matmul(normed_one.T, query_grad)
    key_weight_grad = matmul(normed_one.T, key_grad)
    value_weight_grad = matmul(normed_one.T, value_grad)
    normed_terms_one = (
        matmul(query_grad, query_w.T) + matmul(key_grad, key_w.T) + matmul(value_grad, value_w.T)
    )
    normed_grad_one = lax.psum(normed_terms_one.astype(jnp.bfloat16), "col").astype(jnp.float32)
    rows_norm_grad, attn_gain_grad = norm_back(rows_wide, inv_one, attn_gain, normed_grad_one)
    rows_grad = resid_grad + rows_norm_grad
    input_share = lax.dynamic_slice_in_dim(rows_grad, col_start, quarter, 1).astype(jnp.bfloat16)
    (
        query_result,
        key_result,
        value_result,
        output_result,
        gate_result,
        up_result,
        down_result,
        attn_gain_result,
        ffn_gain_result,
    ) = scatter_rows(
        [
            query_weight_grad,
            key_weight_grad,
            value_weight_grad,
            output_weight_grad,
            gate_weight_grad,
            up_weight_grad,
            down_weight_grad,
            attn_gain_grad,
            ffn_gain_grad,
        ]
    )
    back_rows, back_grads = (
        lax.all_to_all(output_share[arrived_slots], "row", split_axis=0, concat_axis=0, tiled=True),
        lax.all_to_all(input_share[arrived_slots], "row", split_axis=0, concat_axis=0, tiled=True),
    )
    restore = jnp.argsort(send_order)
    return (
        back_rows[restore],
        back_grads[restore],
        attn_gain_result,
        query_result,
        key_result,
        value_result,
        output_result,
        ffn_gain_result,
        gate_result,
        up_result,
        down_result,
    )


def solution(mesh):
    placed = (
        P("row", "col"),
        P("row", "col"),
        P("row"),
        P("row"),
        P(),
        P("row", "col"),
        P("row", "col"),
        P("row", "col"),
        P("row", "col"),
        P(),
        P("row", "col"),
        P("row", "col"),
        P("row", "col"),
    )
    return jax.shard_map(
        body,
        mesh=mesh,
        in_specs=placed,
        out_specs=(
            P("row", "col"),
            P("row", "col"),
            P("row"),
            P("row", "col"),
            P("row", "col"),
            P("row", "col"),
            P("row", "col"),
            P("row"),
            P("row", "col"),
            P("row", "col"),
            P("row", "col"),
        ),
        check_vma=False,
    )
```

profile of v0, /device:TPU:1, one launch (start us, length us, event | category | flops | bytes accessed | tf_op | source)
XLA Modules:
  0.0 914.6 jit_solution(13303859457156370730)
XLA Ops:
  16.6 9.6 %all-to-all-start.1 = ((s32[32,16,1]{1,2,0:T(1,128)}), s32[32,16,1]{1,2,0:T(1,128)S(1)}, u32[]{:S(2)}, u32[]{:S(2)}) async-start(s32[32,16,1]{1,2,0:T(1,128)} %bitcast.2), calls=%async_computation.1 | async-start | bytes 32768 | tf_op jit(solution)/shard_map/all_to_all | solution.py:147
  42.4 6.5 all-to-all-done
  53.7 26.4 %all-gather.11.cloned.1.call-done = bf16[512,2048]{1,0:T(8,128)(2,1)} async-done(((bf16[512,512]{1,0:T(8,128)(2,1)}), bf16[512,2048]{1,0:T(8,128)(2,1)}) %all-gather.11.cloned.1.call-update) | async-done | bytes 2097168 | tf_op jit(solution)/shard_map/all_gather | solution.py:151
  82.1 48.2 %all-gather.7.cloned.1.call-done = bf16[2048,1152]{1,0:T(8,128)(2,1)} async-done(((bf16[64,1152]{1,0:T(8,128)(2,1)}), bf16[2048,1152]{1,0:T(8,128)(2,1)}) %all-gather.7.cloned.1.call-update) | async-done | bytes 4718608 | tf_op jit(solution)/shard_map/all_gather | solution.py:99
  140.1 25.1 %while.32 = (s32[]{:T(128)}, bf16[8,512,64]{1,2,0:T(8,128)(2,1)S(1)}, f32[8,512]{1,0:T(8,128)}, bf16[8,512,64]{2,1,0:T(8,128)(2,1)}, bf16[1,512,64]{2,1,0:T(8,12...) while((s32[]{:T(128)}, bf16[8,512,64]{1,2,0:T(8,128)(2,1)S(1)}, ...), condition=%wide.region_8.9_spmd.clone.clone, body=%wide.region_5.8_spmd.clone.sunk.clone | while | flops 69991936 | bytes 3694689 | solution.py:178
  174.0 16.6 %all_to_all.60 = bf16[32,16,512]{2,1,0:T(8,128)(2,1)S(1)} all-to-all(bf16[32,16,512]{2,1,0:T(8,128)(2,1)S(1)} %bitcast.184), channel_id=1, replica_groups=mesh['row'=32,'col'=4] {'row'}, dimensions={0} | all-to-all | bytes 1048576 | tf_op jit(solution)/shard_map/all_to_all | solution.py:146
  195.2 67.6 %all-reduce.4.cloned.1.call-done = f32[512,2048]{1,0:T(8,128)} async-done(((f32[512,2048]{1,0:T(8,128)}), f32[512,2048]{1,0:T(8,128)}) %all-reduce.4.cloned.1.call-update) | async-done | bytes 4194320 | tf_op jit(solution)/shard_map/psum | solution.py:194
  269.3 26.3 %all-gather.13.cloned.1.call-done = bf16[512,2048]{1,0:T(8,128)(2,1)} async-done(((bf16[512,512]{1,0:T(8,128)(2,1)}), bf16[512,2048]{1,0:T(8,128)(2,1)}) %all-gather.13.cloned.1.call-update) | async-done | bytes 2097168 | tf_op jit(solution)/shard_map/all_gather | solution.py:152
  295.7 76.7 %all-gather.9.cloned.1.call-done = bf16[2048,4224]{1,0:T(8,128)(2,1)} async-done(((bf16[64,4224]{1,0:T(8,128)(2,1)}), bf16[2048,4224]{1,0:T(8,128)(2,1)}) %all-gather.9.cloned.1.call-update) | async-done | bytes 17301520 | tf_op jit(solution)/shard_map/all_gather | solution.py:99
  372.4 6.5 fusion.41
  386.2 7.3 multiply_convert_fusion.4
  393.6 5.4 fusion.45
  404.0 9.7 %all-reduce.8.cloned.1.call-start = ((), (), s32[]{:S(2)}) async-start(), calls=%async_computation.12 | async-start | bytes 4194304 | tf_op jit(solution)/shard_map/psum | solution.py:253
  413.7 82.1 %all-reduce.6.cloned.1.call-done = f32[512,2048]{1,0:T(8,128)} async-done(((f32[512,2048]{1,0:T(8,128)}), f32[512,2048]{1,0:T(8,128)}) %all-reduce.6.cloned.1.call-update) | async-done | bytes 4194320 | tf_op jit(solution)/shard_map/psum | solution.py:217
  511.6 50.9 %while.33 = (s32[]{:T(128)}, f32[8,512,64]{1,2,0:T(8,128)}, f32[8,512,64]{1,2,0:T(8,128)}, f32[8,512,64]{1,2,0:T(8,128)}, bf16[8,512,64]{2,1,0:T(8,128)(2,1)}, /...) while((s32[]{:T(128)}, f32[8,512,64]{1,2,0:T(8,128)}, ...), condition=%wide.region_17.18_spmd.clone.clone, body=%wide.region_15.17_spmd.clone.sunk.clone | while | flops 170982912 | bytes 9126013 | solution.py:224
  575.5 7.9 fusion.58
  583.5 7.9 convolution_convert_fusion.2
  608.7 25.4 %all-reduce.8.cloned.1.call-done = bf16[512,2048]{1,0:T(8,128)(2,1)} async-done(((bf16[512,2048]{1,0:T(8,128)(2,1)}), bf16[512,2048]{1,0:T(8,128)(2,1)}) %all-reduce.8.cloned.1.call-update) | async-done | bytes 2097168 | tf_op jit(solution)/shard_map/psum | solution.py:253
  634.1 6.1 fusion.53
  640.2 93.2 %concatenate.53 = bf16[2048,5378]{0,1:T(8,128)(2,1)} concatenate(bf16[2048,512]{0,1:T(8,128)(2,1)} %convolution_convert_fusion.4, bf16[2048,64]{0,1:T(8,128)(2,1)S(1)} %convolution_convert_fusion.6, bf16[2048,64]{0,1:T(8,128)(2,1)S(1)} %convolution_convert_fusion.5, bf16[2048,512]{0,1:T(8,128)(2,1)} %convolution_convert_fusion.3, bf16[2048,1408]{0,1:T(8,128)(2,1)} %convolution_convert_fusion.2, ...), dimensions={1} | concatenate | bytes 44056576 | tf_op jit(solution)/shard_map/concatenate | solution.py:112
  733.5 28.4 %copy.67 = bf16[2048,5378]{1,0:T(8,128)(2,1)} copy(bf16[2048,5378]{0,1:T(8,128)(2,1)} %concatenate.53) | data formatting | bytes 44056576
  766.9 7.7 all-to-all-start.2
  779.8 6.4 all-to-all-done.2
  804.7 89.5 %reduce-scatter.7.cloned.1.call-done = bf16[64,5378]{1,0:T(8,128)(2,1)} async-done(((bf16[2048,5378]{1,0:T(8,128)(2,1)}), bf16[64,5378]{1,0:T(8,128)(2,1)}) %reduce-scatter.7.cloned.1.call-update) | async-done | bytes 688400
  (288 shorter events, 238.0 us)
Async XLA Ops:
  7.2 19.0 %copy-start = (bf16[512,512]{1,0:T(8,128)(2,1)S(1)}, bf16[512,512]{1,0:T(8,128)(2,1)}, u32[]{:S(2)}) copy-start(bf16[512,512]{1,0:T(8,128)(2,1)} %param.17) | copy-start | bytes 1572868
  16.6 16.5 %all-to-all-start.1 = ((s32[32,16,1]{1,2,0:T(1,128)}), s32[32,16,1]{1,2,0:T(1,128)S(1)}, u32[]{:S(2)}, u32[]{:S(2)}) async-start(s32[32,16,1]{1,2,0:T(1,128)} %bitcast.2), calls=%async_computation.1 | async-start | bytes 32768 | tf_op jit(solution)/shard_map/all_to_all | solution.py:147
  28.9 22.8 %copy-start.19 = (bf16[64,512]{1,0:T(8,128)(2,1)S(1)}, bf16[64,512]{1,0:T(8,128)(2,1)}, u32[]{:S(2)}) copy-start(bf16[64,512]{1,0:T(8,128)(2,1)} %param.22) | copy-start | bytes 196612
  28.9 22.8 %copy-start.20 = (bf16[64,512]{1,0:T(8,128)(2,1)S(1)}, bf16[64,512]{1,0:T(8,128)(2,1)}, u32[]{:S(2)}) copy-start(bf16[64,512]{1,0:T(8,128)(2,1)} %param.25) | copy-start | bytes 196612
  28.9 22.8 %copy-start.21 = (bf16[64,64]{1,0:T(8,128)(2,1)S(1)}, bf16[64,64]{1,0:T(8,128)(2,1)}, u32[]{:S(2)}) copy-start(bf16[64,64]{1,0:T(8,128)(2,1)} %param.23) | copy-start | bytes 24580
  28.9 22.8 %copy-start.22 = (bf16[64,64]{1,0:T(8,128)(2,1)S(1)}, bf16[64,64]{1,0:T(8,128)(2,1)}, u32[]{:S(2)}) copy-start(bf16[64,64]{1,0:T(8,128)(2,1)} %param.24) | copy-start | bytes 24580
  28.9 23.7 %copy-start.25 = (s32[512]{0:T(512)S(1)}, s32[512]{0:T(512)}, u32[]{:S(2)}) copy-start(s32[512]{0:T(512)} %param.20) | copy-start | bytes 6148
  33.1 49.0 %copy-start.16 = (s32[32,16,1]{1,2,0:T(1,128)}, s32[32,16,1]{1,2,0:T(1,128)S(1)}, u32[]{:S(2)}) copy-start(s32[32,16,1]{1,2,0:T(1,128)S(1)} %all-to-all-done.1) | copy-start | bytes 6148
  33.1 15.9 %all-to-all-start = ((bf16[32,16,512]{2,1,0:T(8,128)(2,1)}), bf16[32,16,512]{2,1,0:T(8,128)(2,1)S(1)}, u32[]{:S(2)}, u32[]{:S(2)}) async-start(bf16[32,16,512]{2,1,0:T(8,128)(2,1)} %bitcast), calls=%async_computation | async-start | bytes 1048576 | tf_op jit(solution)/shard_map/all_to_all | solution.py:145
  37.3 42.7 %all-gather.11.cloned.1.call-start = ((), (), s32[]{:S(2)}) async-start(), calls=%async_computation.13 | async-start | bytes 2621440 | tf_op jit(solution)/shard_map/all_gather | solution.py:151
  48.9 81.4 %copy-start.23 = (f32[2048]{0:T(1024)S(1)}, f32[2048]{0:T(1024)}, u32[]{:S(2)}) copy-start(f32[2048]{0:T(1024)} %param.21) | copy-start | bytes 24580
  51.6 78.8 %all-gather.7.cloned.1.call-start = ((), (), s32[]{:S(2)}) async-start(), calls=%async_computation.7 | async-start | bytes 4866048 | tf_op jit(solution)/shard_map/all_gather | solution.py:99
  52.5 210.3 %all-reduce.4.cloned.1.call-start = ((), (), s32[]{:S(2)}) async-start(), calls=%async_computation.8 | async-start | bytes 8388608 | tf_op jit(solution)/shard_map/psum | solution.py:194
  53.1 84.4 %copy-start.30 = (f32[32]{0:T(128)}, f32[32]{0:T(128)S(1)}, u32[]{:S(2)}) copy-start(f32[32]{0:T(128)S(1)} %negate_power_fusion) | copy-start | bytes 388
  171.0 124.6 %all-gather.13.cloned.1.call-start = ((), (), s32[]{:S(2)}) async-start(), calls=%async_computation.14 | async-start | bytes 2621440 | tf_op jit(solution)/shard_map/all_gather | solution.py:152
  193.3 179.1 %all-gather.9.cloned.1.call-start = ((), (), s32[]{:S(2)}) async-start(), calls=%async_computation.9 | async-start | bytes 17842176 | tf_op jit(solution)/shard_map/all_gather | solution.py:99
  195.1 72.5 %copy-start.18 = (f32[2048]{0:T(1024)S(1)}, f32[2048]{0:T(1024)}, u32[]{:S(2)}) copy-start(f32[2048]{0:T(1024)} %param.26) | copy-start | bytes 24580
  195.1 300.7 %all-reduce.6.cloned.1.call-start = ((), (), s32[]{:S(2)}) async-start(), calls=%async_computation.11 | async-start | bytes 8388608 | tf_op jit(solution)/shard_map/psum | solution.py:217
  404.0 230.1 %all-reduce.8.cloned.1.call-start = ((), (), s32[]{:S(2)}) async-start(), calls=%async_computation.12 | async-start | bytes 4194304 | tf_op jit(solution)/shard_map/psum | solution.py:253
  575.4 187.3 %reduce-scatter.5.cloned.1.call-start = ((), (), s32[]{:S(2)}) async-start(), calls=%async_computation.10 | async-start | bytes 2621440 | tf_op jit(solution)/shard_map/reduce_scatter | solution.py:204
  583.4 310.8 %reduce-scatter.7.cloned.1.call-start = ((), (), s32[]{:S(2)}) async-start(), calls=%async_computation.15 | async-start | bytes 23248896
  766.9 19.3 %all-to-all-start.2 = ((bf16[32,16,512]{2,1,0:T(8,128)(2,1)}), bf16[32,16,512]{2,1,0:T(8,128)(2,1)S(1)}, u32[]{:S(2)}, u32[]{:S(2)}) async-start(bf16[32,16,512]{2,1,0:T(8,128)(2,1)} %bitcast.14), calls=%async_computation.3 | async-start | bytes 1048576 | tf_op jit(solution)/shard_map/all_to_all | solution.py:281
  774.6 15.9 %copy-start.29 = (s32[512]{0:T(512)S(1)}, s32[512]{0:T(512)}, u32[]{:S(2)}) copy-start(s32[512]{0:T(512)} %copy-done.28) | copy-start | bytes 6148
  786.1 15.9 %all-to-all-start.4 = ((bf16[32,16,512]{2,1,0:T(8,128)(2,1)}), bf16[32,16,512]{2,1,0:T(8,128)(2,1)S(1)}, u32[]{:S(2)}, u32[]{:S(2)}) async-start(bf16[32,16,512]{2,1,0:T(8,128)(2,1)} %bitcast.24), calls=%async_computation.5 | async-start | bytes 1048576 | tf_op jit(solution)/shard_map/all_to_all | solution.py:282
  (24 other events, 102.9 us)
Sparse Core Ops, SparseCore 0:
  51.7 28.2 all-gather.10
  82.8 47.4 all-gather.6
  171.1 91.5 all-reduce.3
  264.9 30.6 all-gather.12
  298.0 74.3 all-gather.8
  404.1 91.7 all-reduce.5
  575.6 58.4 all-reduce.7
  636.6 29.4 reduce-scatter.4
  762.0 132.1 reduce-scatter.6
where the time goes:
time: 928 us; the launch traced here: 915 us
  waiting for transfers between devices  465 us (50%)
  local copies, waits for them, and re-layouts  191 us (21%)
  matrix products  142 us (15%)
  other arithmetic  49.6 us (5%)
  starting transfers between devices  36.1 us (4%)
  blocking collectives  16.6 us (2%)
  between operations  14.9 us (2%)
    dot_general x77, matrix products, matmul(): return jnp.dot(left, right, preferred_element_type=jnp.float32)  142 us
    all_gather x2, waiting for transfers between devices, gather_rows(): lax.all_gather(jnp.concatenate(parts, axis=1), 'row', axis=0, tiled=True)  125 us
    concatenate x1, local copies, waits for them, and re-layouts, scatter_rows(): jnp.concatenate(columns, axis=1)  93.2 us
    unnamed x10, waiting for transfers between devices  89.6 us
    psum x1, waiting for transfers between devices, body(): normed_grad_two = lax.psum(normed_terms_two, 'col')  82.1 us
    psum x1, waiting for transfers between devices, body(): attn_full = lax.psum(attn_terms, 'col')  67.6 us
    unnamed x82, local copies, waits for them, and re-layouts  51.5 us
    all_gather x1, waiting for transfers between devices, body(): lax.all_gather(arrived_rows[placing], 'col', axis=1, tiled=True)  26.4 us
  transfers between devices with their start and end apart: 13, of which 12 were waited for; matrix products, arithmetic and copies ran while one was open for 22% of the time, Pallas kernels for 0%

commit v1 on v0

--- a/solution.py
+++ b/solution.py
@@ -250,7 +250,9 @@
     normed_terms_one = (
         matmul(query_grad, query_w.T) + matmul(key_grad, key_w.T) + matmul(value_grad, value_w.T)
     )
-    normed_grad_one = lax.psum(normed_terms_one.astype(jnp.bfloat16), "col").astype(jnp.float32)
+    normed_grad_one = jnp.sum(
+        jax.lax.all_gather(normed_terms_one.astype(jnp.bfloat16), axis_name="col"), 0
+    ).astype(jnp.float32)
     rows_norm_grad, attn_gain_grad = norm_back(rows_wide, inv_one, attn_gain, normed_grad_one)
     rows_grad = resid_grad + rows_norm_grad
     input_share = lax.dynamic_slice_in_dim(rows_grad, col_start, quarter, 1).astype(jnp.bfloat16)

time: 928 us -> 961 us (1.036)
  waiting for transfers between devices: 465 us -> 490 us
    all_gather x0 -> x1, waiting for transfers between devices: none -> 49.5 us  [body(): jax.lax.all_gather(normed_terms_one.astype(jnp.bfloat16), axis_name='col')]
    psum x1 -> x0, waiting for transfers between devices: 25.4 us -> none  [body(): lax.psum(normed_terms_one.astype(jnp.bfloat16), 'col').astype(jnp.float32)]
    all_gather x0 -> x1, starting transfers between devices: none -> 9.71 us  [body(): jax.lax.all_gather(normed_terms_one.astype(jnp.bfloat16), axis_name='col')]
    psum x1 -> x0, starting transfers between devices: 9.71 us -> none  [body(): lax.psum(normed_terms_one.astype(jnp.bfloat16), 'col').astype(jnp.float32)]
where the time goes in v1:
time: 961 us; the launch traced here: 948 us
  waiting for transfers between devices  490 us (51%)
  local copies, waits for them, and re-layouts  191 us (20%)
  matrix products  142 us (15%)
  other arithmetic  56.9 us (6%)
  starting transfers between devices  35.8 us (4%)
  blocking collectives  16.6 us (2%)
  between operations  14.9 us (2%)
    dot_general x77, matrix products, matmul(): return jnp.dot(left, right, preferred_element_type=jnp.float32)  142 us
    all_gather x2, waiting for transfers between devices, gather_rows(): lax.all_gather(jnp.concatenate(parts, axis=1), 'row', axis=0, tiled=True)  125 us
    concatenate x1, local copies, waits for them, and re-layouts, scatter_rows(): jnp.concatenate(columns, axis=1)  93.2 us
    unnamed x10, waiting for transfers between devices  90.8 us
    psum x1, waiting for transfers between devices, body(): normed_grad_two = lax.psum(normed_terms_two, 'col')  82.1 us
    psum x1, waiting for transfers between devices, body(): attn_full = lax.psum(attn_terms, 'col')  67.5 us
    unnamed x82, local copies, waits for them, and re-layouts  51.5 us
    all_gather x1, waiting for transfers between devices, body(): jax.lax.all_gather(normed_terms_one.astype(jnp.bfloat16), axis_name='col')  49.5 us
  transfers between devices with their start and end apart: 13, of which 12 were waited for; matrix products, arithmetic and copies ran while one was open for 22% of the time, Pallas kernels for 0%

profile of v1, /device:TPU:1, one launch (start us, length us, event | category | flops | bytes accessed | tf_op | source)
XLA Modules:
  0.0 947.6 jit_solution(14010568968681377162)
XLA Ops:
  16.6 9.6 %all-to-all-start.1 = ((s32[32,16,1]{1,2,0:T(1,128)}), s32[32,16,1]{1,2,0:T(1,128)S(1)}, u32[]{:S(2)}, u32[]{:S(2)}) async-start(s32[32,16,1]{1,2,0:T(1,128)} %bitcast.2), calls=%async_computation.1 | async-start | bytes 32768 | tf_op jit(solution)/shard_map/all_to_all | solution.py:147
  42.4 6.5 all-to-all-done
  53.7 26.4 %all-gather.13.cloned.1.call-done = bf16[512,2048]{1,0:T(8,128)(2,1)} async-done(((bf16[512,512]{1,0:T(8,128)(2,1)}), bf16[512,2048]{1,0:T(8,128)(2,1)}) %all-gather.13.cloned.1.call-update) | async-done | bytes 2097168 | tf_op jit(solution)/shard_map/all_gather | solution.py:151
  82.1 48.2 %all-gather.9.cloned.1.call-done = bf16[2048,1152]{1,0:T(8,128)(2,1)} async-done(((bf16[64,1152]{1,0:T(8,128)(2,1)}), bf16[2048,1152]{1,0:T(8,128)(2,1)}) %all-gather.9.cloned.1.call-update) | async-done | bytes 4718608 | tf_op jit(solution)/shard_map/all_gather | solution.py:99
  140.1 25.1 %while.32 = (s32[]{:T(128)}, bf16[8,512,64]{1,2,0:T(8,128)(2,1)S(1)}, f32[8,512]{1,0:T(8,128)}, bf16[8,512,64]{2,1,0:T(8,128)(2,1)}, bf16[1,512,64]{2,1,0:T(8,12...) while((s32[]{:T(128)}, bf16[8,512,64]{1,2,0:T(8,128)(2,1)S(1)}, ...), condition=%wide.region_8.9_spmd.clone.clone, body=%wide.region_5.8_spmd.clone.sunk.clone | while | flops 69991936 | bytes 3694689 | solution.py:178
  174.0 16.6 %all_to_all.60 = bf16[32,16,512]{2,1,0:T(8,128)(2,1)S(1)} all-to-all(bf16[32,16,512]{2,1,0:T(8,128)(2,1)S(1)} %bitcast.186), channel_id=1, replica_groups=mesh['row'=32,'col'=4] {'row'}, dimensions={0} | all-to-all | bytes 1048576 | tf_op jit(solution)/shard_map/all_to_all | solution.py:146
  195.2 67.5 %all-reduce.3.cloned.1.call-done = f32[512,2048]{1,0:T(8,128)} async-done(((f32[512,2048]{1,0:T(8,128)}), f32[512,2048]{1,0:T(8,128)}) %all-reduce.3.cloned.1.call-update) | async-done | bytes 4194320 | tf_op jit(solution)/shard_map/psum | solution.py:194
  269.3 26.3 %all-gather.15.cloned.1.call-done = bf16[512,2048]{1,0:T(8,128)(2,1)} async-done(((bf16[512,512]{1,0:T(8,128)(2,1)}), bf16[512,2048]{1,0:T(8,128)(2,1)}) %all-gather.15.cloned.1.call-update) | async-done | bytes 2097168 | tf_op jit(solution)/shard_map/all_gather | solution.py:152
  295.7 76.7 %all-gather.11.cloned.1.call-done = bf16[2048,4224]{1,0:T(8,128)(2,1)} async-done(((bf16[64,4224]{1,0:T(8,128)(2,1)}), bf16[2048,4224]{1,0:T(8,128)(2,1)}) %all-gather.11.cloned.1.call-update) | async-done | bytes 17301520 | tf_op jit(solution)/shard_map/all_gather | solution.py:99
  372.4 6.5 fusion.41
  386.2 7.3 multiply_convert_fusion.4
  404.0 9.7 %all-gather.17.cloned.1.call-start = ((), (), s32[]{:S(2)}) async-start(), calls=%async_computation.14 | async-start | bytes 10485760 | tf_op jit(solution)/shard_map/all_gather | solution.py:254
  413.7 82.1 %all-reduce.5.cloned.1.call-done = f32[512,2048]{1,0:T(8,128)} async-done(((f32[512,2048]{1,0:T(8,128)}), f32[512,2048]{1,0:T(8,128)}) %all-reduce.5.cloned.1.call-update) | async-done | bytes 4194320 | tf_op jit(solution)/shard_map/psum | solution.py:217
  511.6 50.9 %while.33 = (s32[]{:T(128)}, f32[8,512,64]{1,2,0:T(8,128)}, f32[8,512,64]{1,2,0:T(8,128)}, f32[8,512,64]{1,2,0:T(8,128)}, bf16[8,512,64]{2,1,0:T(8,128)(2,1)}, /...) while((s32[]{:T(128)}, f32[8,512,64]{1,2,0:T(8,128)}, ...), condition=%wide.region_17.18_spmd.clone.clone, body=%wide.region_15.17_spmd.clone.sunk.clone | while | flops 170982912 | bytes 9126013 | solution.py:224
  575.5 7.9 fusion.58
  583.5 8.3 convolution_convert_fusion.2
  609.1 49.5 %all-gather.17.cloned.1.call-done = bf16[2048,2048]{1,0:T(8,128)(2,1)} async-done(((bf16[512,2048]{1,0:T(8,128)(2,1)}), bf16[2048,2048]{1,0:T(8,128)(2,1)}) %all-gather.17.cloned.1.call-update) | async-done | bytes 8388624 | tf_op jit(solution)/shard_map/all_gather | solution.py:254
  658.6 7.2 reduce_sum.109
  665.8 6.2 fusion.53
  672.0 93.2 %concatenate.53 = bf16[2048,5378]{0,1:T(8,128)(2,1)} concatenate(bf16[2048,512]{0,1:T(8,128)(2,1)} %convolution_convert_fusion.4, bf16[2048,64]{0,1:T(8,128)(2,1)S(1)} %convolution_convert_fusion.6, bf16[2048,64]{0,1:T(8,128)(2,1)S(1)} %convolution_convert_fusion.5, bf16[2048,512]{0,1:T(8,128)(2,1)} %convolution_convert_fusion.3, bf16[2048,1408]{0,1:T(8,128)(2,1)} %convolution_convert_fusion.2, ...), dimensions={1} | concatenate | bytes 44056576 | tf_op jit(solution)/shard_map/concatenate | solution.py:112
  765.2 28.4 %copy.67 = bf16[2048,5378]{1,0:T(8,128)(2,1)} copy(bf16[2048,5378]{0,1:T(8,128)(2,1)} %concatenate.53) | data formatting | bytes 44056576
  798.9 7.7 all-to-all-start.2
  811.7 6.4 all-to-all-done.2
  836.4 90.7 %reduce-scatter.7.cloned.1.call-done = bf16[64,5378]{1,0:T(8,128)(2,1)} async-done(((bf16[2048,5378]{1,0:T(8,128)(2,1)}), bf16[64,5378]{1,0:T(8,128)(2,1)}) %reduce-scatter.7.cloned.1.call-update) | async-done | bytes 688400
  (289 shorter events, 243.4 us)
Async XLA Ops:
  7.2 19.0 %copy-start = (bf16[512,512]{1,0:T(8,128)(2,1)S(1)}, bf16[512,512]{1,0:T(8,128)(2,1)}, u32[]{:S(2)}) copy-start(bf16[512,512]{1,0:T(8,128)(2,1)} %param.17) | copy-start | bytes 1572868
  16.6 16.5 %all-to-all-start.1 = ((s32[32,16,1]{1,2,0:T(1,128)}), s32[32,16,1]{1,2,0:T(1,128)S(1)}, u32[]{:S(2)}, u32[]{:S(2)}) async-start(s32[32,16,1]{1,2,0:T(1,128)} %bitcast.2), calls=%async_computation.1 | async-start | bytes 32768 | tf_op jit(solution)/shard_map/all_to_all | solution.py:147
  28.9 22.8 %copy-start.19 = (bf16[64,512]{1,0:T(8,128)(2,1)S(1)}, bf16[64,512]{1,0:T(8,128)(2,1)}, u32[]{:S(2)}) copy-start(bf16[64,512]{1,0:T(8,128)(2,1)} %param.22) | copy-start | bytes 196612
  28.9 22.8 %copy-start.20 = (bf16[64,512]{1,0:T(8,128)(2,1)S(1)}, bf16[64,512]{1,0:T(8,128)(2,1)}, u32[]{:S(2)}) copy-start(bf16[64,512]{1,0:T(8,128)(2,1)} %param.25) | copy-start | bytes 196612
  28.9 22.8 %copy-start.21 = (bf16[64,64]{1,0:T(8,128)(2,1)S(1)}, bf16[64,64]{1,0:T(8,128)(2,1)}, u32[]{:S(2)}) copy-start(bf16[64,64]{1,0:T(8,128)(2,1)} %param.23) | copy-start | bytes 24580
  28.9 22.8 %copy-start.22 = (bf16[64,64]{1,0:T(8,128)(2,1)S(1)}, bf16[64,64]{1,0:T(8,128)(2,1)}, u32[]{:S(2)}) copy-start(bf16[64,64]{1,0:T(8,128)(2,1)} %param.24) | copy-start | bytes 24580
  28.9 23.7 %copy-start.25 = (s32[512]{0:T(512)S(1)}, s32[512]{0:T(512)}, u32[]{:S(2)}) copy-start(s32[512]{0:T(512)} %param.20) | copy-start | bytes 6148
  33.1 49.0 %copy-start.16 = (s32[32,16,1]{1,2,0:T(1,128)}, s32[32,16,1]{1,2,0:T(1,128)S(1)}, u32[]{:S(2)}) copy-start(s32[32,16,1]{1,2,0:T(1,128)S(1)} %all-to-all-done.1) | copy-start | bytes 6148
  33.1 15.9 %all-to-all-start = ((bf16[32,16,512]{2,1,0:T(8,128)(2,1)}), bf16[32,16,512]{2,1,0:T(8,128)(2,1)S(1)}, u32[]{:S(2)}, u32[]{:S(2)}) async-start(bf16[32,16,512]{2,1,0:T(8,128)(2,1)} %bitcast), calls=%async_computation | async-start | bytes 1048576 | tf_op jit(solution)/shard_map/all_to_all | solution.py:145
  37.3 42.7 %all-gather.13.cloned.1.call-start = ((), (), s32[]{:S(2)}) async-start(), calls=%async_computation.12 | async-start | bytes 2621440 | tf_op jit(solution)/shard_map/all_gather | solution.py:151
  48.9 81.4 %copy-start.23 = (f32[2048]{0:T(1024)S(1)}, f32[2048]{0:T(1024)}, u32[]{:S(2)}) copy-start(f32[2048]{0:T(1024)} %param.21) | copy-start | bytes 24580
  51.6 78.8 %all-gather.9.cloned.1.call-start = ((), (), s32[]{:S(2)}) async-start(), calls=%async_computation.7 | async-start | bytes 4866048 | tf_op jit(solution)/shard_map/all_gather | solution.py:99
  52.5 210.3 %all-reduce.3.cloned.1.call-start = ((), (), s32[]{:S(2)}) async-start(), calls=%async_computation.8 | async-start | bytes 8388608 | tf_op jit(solution)/shard_map/psum | solution.py:194
  53.1 84.4 %copy-start.30 = (f32[32]{0:T(128)}, f32[32]{0:T(128)S(1)}, u32[]{:S(2)}) copy-start(f32[32]{0:T(128)S(1)} %negate_power_fusion) | copy-start | bytes 388
  171.0 124.6 %all-gather.15.cloned.1.call-start = ((), (), s32[]{:S(2)}) async-start(), calls=%async_computation.13 | async-start | bytes 2621440 | tf_op jit(solution)/shard_map/all_gather | solution.py:152
  193.3 179.1 %all-gather.11.cloned.1.call-start = ((), (), s32[]{:S(2)}) async-start(), calls=%async_computation.9 | async-start | bytes 17842176 | tf_op jit(solution)/shard_map/all_gather | solution.py:99
  195.1 72.5 %copy-start.18 = (f32[2048]{0:T(1024)S(1)}, f32[2048]{0:T(1024)}, u32[]{:S(2)}) copy-start(f32[2048]{0:T(1024)} %param.26) | copy-start | bytes 24580
  195.2 300.7 %all-reduce.5.cloned.1.call-start = ((), (), s32[]{:S(2)}) async-start(), calls=%async_computation.11 | async-start | bytes 8388608 | tf_op jit(solution)/shard_map/psum | solution.py:217
  404.0 254.6 %all-gather.17.cloned.1.call-start = ((), (), s32[]{:S(2)}) async-start(), calls=%async_computation.14 | async-start | bytes 10485760 | tf_op jit(solution)/shard_map/all_gather | solution.py:254
  575.5 219.0 %reduce-scatter.5.cloned.1.call-start = ((), (), s32[]{:S(2)}) async-start(), calls=%async_computation.10 | async-start | bytes 2621440 | tf_op jit(solution)/shard_map/reduce_scatter | solution.py:204
  583.4 343.7 %reduce-scatter.7.cloned.1.call-start = ((), (), s32[]{:S(2)}) async-start(), calls=%async_computation.15 | async-start | bytes 23248896
  798.9 19.3 %all-to-all-start.2 = ((bf16[32,16,512]{2,1,0:T(8,128)(2,1)}), bf16[32,16,512]{2,1,0:T(8,128)(2,1)S(1)}, u32[]{:S(2)}, u32[]{:S(2)}) async-start(bf16[32,16,512]{2,1,0:T(8,128)(2,1)} %bitcast.14), calls=%async_computation.3 | async-start | bytes 1048576 | tf_op jit(solution)/shard_map/all_to_all | solution.py:283
  806.6 15.6 %copy-start.29 = (s32[512]{0:T(512)S(1)}, s32[512]{0:T(512)}, u32[]{:S(2)}) copy-start(s32[512]{0:T(512)} %copy-done.28) | copy-start | bytes 6148
  818.1 15.7 %all-to-all-start.4 = ((bf16[32,16,512]{2,1,0:T(8,128)(2,1)}), bf16[32,16,512]{2,1,0:T(8,128)(2,1)S(1)}, u32[]{:S(2)}, u32[]{:S(2)}) async-start(bf16[32,16,512]{2,1,0:T(8,128)(2,1)} %bitcast.25), calls=%async_computation.5 | async-start | bytes 1048576 | tf_op jit(solution)/shard_map/all_to_all | solution.py:284
  (24 other events, 103.6 us)
Sparse Core Ops, SparseCore 0:
  51.7 28.2 all-gather.12
  82.8 47.4 all-gather.8
  171.1 91.5 all-reduce.2
  264.9 30.6 all-gather.14
  298.0 74.3 all-gather.10
  404.1 91.7 all-reduce.4
  575.6 82.9 all-gather.16
  661.0 30.6 reduce-scatter.4
  793.8 133.3 reduce-scatter.6
